TPU v7x, 256 devices: a whole 4x4x8 slice. The times are simulated.
256 devices in a mesh: seq: 64 (over y, z, core), head: 4 (over x).
Axes of the slice: x: 4, y: 4, z: 8, core: 2. Of those that a mesh axis runs over, the one named last changes fastest.
Arguments:
- queries: bfloat16 [32768, 2048], P('seq', 'head'), may hold values from -6 to 6
- keys: bfloat16 [32768, 2048], P('seq', 'head'), may hold values from -6 to 6
- values: bfloat16 [32768, 2048], P('seq', 'head'), may hold values from -6 to 6
- out_grad: bfloat16 [32768, 4096], P('seq', 'head'), may hold values from -16 to 16
- out_weight: bfloat16 [4096, 2048], P(None, 'head'), may hold values from -0.125 to 0.125
Outputs:
- query_grad: bfloat16 [32768, 2048], P('seq', 'head')
- key_grad: bfloat16 [32768, 2048], P('seq', 'head')
- value_grad: bfloat16 [32768, 2048], P('seq', 'head')
- weight_grad: float32 [4096, 2048], P('seq', 'head')
All inputs are finite; a program needn't handle non-finite values.
Results may differ from a plain program's by a relative error of at most 0.0058.
Values may be sent and summed in bfloat16 or wider, within the bound.
A program may use at most 128 MiB of HBM per device.

v0:
```python
import math
import jax
import jax.numpy as jnp
from jax import lax
from jax.sharding import PartitionSpec as P

HD = 128


def prefix(shard, axis, combine, identity):
    length, mine = (lax.axis_size(axis), lax.axis_index(axis))
    everything = lax.all_gather(shard, axis)
    start = jnp.broadcast_to(jnp.asarray(identity, shard.dtype), shard.shape)

    def turn(k, before):
        at = length - 1 - k
        reached = at > mine
        new = combine(before, everything[at])
        return jnp.where(reached, new, before)

    return lax.fori_loop(0, length, turn, start)


def add_states(earlier, later_part):
    return earlier + later_part


def per_device(queries, keys, values, out_grad, out_weight):
    rows = queries.shape[0]
    local_heads = queries.shape[1] // HD
    total = lax.axis_size("seq") * rows
    scale = 1.0 / math.sqrt(HD * total)
    full_grad = lax.all_gather(out_grad, "head", axis=1, tiled=True)
    attn_grad = jnp.dot(full_grad, out_weight, preferred_element_type=jnp.float32).astype(
        jnp.bfloat16
    )
    shape = (rows, local_heads, HD)
    query = queries.reshape(shape)
    key = keys.reshape(shape)
    value = values.reshape(shape)
    dout = attn_grad.reshape(shape)
    kv_term = scale * jnp.einsum("tha,thb->hab", key, value, preferred_element_type=jnp.float32)
    back_term = scale * jnp.einsum("tha,thb->hab", query, dout, preferred_element_type=jnp.float32)
    zeros = jnp.zeros_like(kv_term)
    position = lax.axis_index("seq")
    piece = lax.all_gather(kv_term[None], "seq", axis=0, tiled=True)
    index = jnp.arange(piece.shape[0], dtype=jnp.int32)
    keep = (index < position).astype(jnp.float32)
    prior_sum = jnp.sum(piece * keep[:, None, None, None], axis=0)
    later_sum = prefix(back_term, "seq", add_states, zeros)
    prior = prior_sum.astype(jnp.bfloat16)
    later = later_sum.astype(jnp.bfloat16)
    mask = jnp.tril(jnp.ones((rows, rows), jnp.float32))
    probs = (
        scale * jnp.einsum("tha,sha->hts", query, key, preferred_element_type=jnp.float32) * mask
    ).astype(jnp.bfloat16)
    grads = (
        scale * jnp.einsum("thb,shb->hts", dout, value, preferred_element_type=jnp.float32) * mask
    ).astype(jnp.bfloat16)
    outputs = (
        jnp.einsum("hts,shb->thb", probs, value, preferred_element_type=jnp.float32)
        + jnp.einsum("tha,hab->thb", query, prior, preferred_element_type=jnp.float32)
    ).astype(jnp.bfloat16)
    query_grad = (
        jnp.einsum("hts,sha->tha", grads, key, preferred_element_type=jnp.float32)
        + jnp.einsum("thb,hab->tha", dout, prior, preferred_element_type=jnp.float32)
    ).astype(jnp.bfloat16)
    key_grad = (
        jnp.einsum("hts,tha->sha", grads, query, preferred_element_type=jnp.float32)
        + jnp.einsum("shb,hab->sha", value, later, preferred_element_type=jnp.float32)
    ).astype(jnp.bfloat16)
    value_grad = (
        jnp.einsum("hts,thb->shb", probs, dout, preferred_element_type=jnp.float32)
        + jnp.einsum("sha,hab->shb", key, later, preferred_element_type=jnp.float32)
    ).astype(jnp.bfloat16)
    flat_out = outputs.reshape(rows, local_heads * HD)
    factor = 1.0 / math.sqrt(total)
    product = lax.dot_general(
        full_grad, flat_out, (((0,), (0,)), ((), ())), preferred_element_type=jnp.float32
    )
    weight_grad = lax.psum_scatter(product * factor, "seq", scatter_dimension=0, tiled=True)
    flat = (rows, local_heads * HD)
    return (query_grad.reshape(flat), key_grad.reshape(flat), value_grad.reshape(flat), weight_grad)


def solution(mesh):
    return jax.shard_map(
        per_device,
        mesh=mesh,
        in_specs=(
            P("seq", "head"),
            P("seq", "head"),
            P("seq", "head"),
            P("seq", "head"),
            P(None, "head"),
        ),
        out_specs=(P("seq", "head"), P("seq", "head"), P("seq", "head"), P("seq", "head")),
        check_vma=False,
    )
```

profile of v0, /device:TPU:2, one launch (start us, length us, event | category | flops | bytes accessed | tf_op | source)
XLA Modules:
  0.0 426.9 jit_solution(13473758385437747828)
XLA Ops:
  8.0 1.3 copy.57
  9.2 2.1 convolution_multiply_fusion.1
  11.4 51.5 %all-gather.6.cloned.1.call-done = bf16[512,4096]{1,0:T(8,128)(2,1)} async-done(((bf16[512,1024]{1,0:T(8,128)(2,1)}), bf16[512,4096]{1,0:T(8,128)(2,1)}) %all-gather.6.cloned.1.call-update) | async-done | bytes 4194320 | tf_op jit(solution)/shard_map/all_gather | solution.py:33
  62.9 5.8 %convolution_convert_fusion = bf16[512,512]{0,1:T(8,128)(2,1)S(1)} fusion(bf16[512,4096]{1,0:T(8,128)(2,1)} %all-gather.6.cloned.1.call-done, bf16[4096,512]{1,0:T(8,128)(2,1)} %param.11), kind=kOutput, calls=%fused_computation.15 | convolution fusion | flops 2147745792 | bytes 8912896 | tf_op jit(solution)/shard_map/dot_general | solution.py:34
  71.0 1.8 convolution_bitcast_fusion.1
  73.5 1.5 convolution_bitcast_fusion
  75.0 1.8 convolution_bitcast_fusion.2
  77.3 89.2 %all-gather.8.cloned.1.call-done = f32[256,128,128]{2,1,0:T(8,128)} async-done(((f32[4,128,128]{2,1,0:T(8,128)}), f32[256,128,128]{2,1,0:T(8,128)}) %all-gather.8.cloned.1.call-update) | async-done | bytes 16777232 | tf_op jit(solution)/shard_map/all_gather | solution.py:46
  166.5 7.7 %multiply_reduce_fusion = bf16[4,128,128]{2,1,0:T(8,128)(2,1)S(1)} fusion(f32[64,4,128,128]{3,2,1,0:T(8,128)} %bitcast.105, f32[64]{0:T(128)S(1)} %compare_convert_fusion), kind=kLoop, calls=%fused_computation.1 | loop fusion | flops 8323072 | bytes 16908544 | tf_op jit(solution)/shard_map/reduce_sum | solution.py:49
  174.3 1.1 fusion.3
  175.4 2.0 copy.47
  177.4 1.6 fusion.6
  179.0 8.0 %multiply_bitcast_fusion = f32[4096,512]{0,1:T(8,128)} fusion(bf16[512,512]{0,1:T(8,128)(2,1)S(1)} %bitcast.114, bf16[512,4096]{1,0:T(8,128)(2,1)} %all-gather.6.cloned.1.call-done), kind=kOutput, calls=%fused_computation.2 | convolution fusion | flops 2149580800 | bytes 13107200 | tf_op jit(solution)/shard_map/dot_general | solution.py:78
  187.0 9.0 %copy.55 = f32[4096,512]{1,0:T(8,128)} copy(f32[4096,512]{0,1:T(8,128)} %multiply_bitcast_fusion) | data formatting | bytes 16777216
  196.0 70.1 %all-gather.10.cloned.1.call-done = f32[256,128,128]{2,1,0:T(8,128)} async-done(((f32[4,128,128]{2,1,0:T(8,128)}), f32[256,128,128]{2,1,0:T(8,128)}) %all-gather.10.cloned.1.call-update) | async-done | bytes 16777232 | tf_op jit(solution)/shard_map/all_gather | solution.py:12
  266.1 68.7 %while.16 = (s32[]{:T(128)}, f32[4,128,128]{2,1,0:T(8,128)S(1)}, s32[]{:T(128)}, f32[64,4,128,128]{3,2,1,0:T(8,128)}, s32[]{:T(128)}, /*index=5*/s32[]{:T(128)}, s32[]{:T(128)}, s32[]{:T(128)}) while((s32[]{:T(128)}, f32[4,128,128]{2,1,0:T(8,128)S(1)}, s32[]{:T(128)}, f32[64,4,128,128]{3,2,1,0:T(8,128)}, s32[]{:T(128)}, ...), condition=%wide.region_2.3_spmd.clone, body=%wide.region_1.2_spmd.clone.sunk | while | flops 196616 | bytes 786595 | solution.py:21
  277.9 1.1 add_select_fusion.2
  288.6 1.1 add_select_fusion.2
  290.8 1.1 add_select_fusion.2
  293.0 1.1 add_select_fusion.2
  311.3 1.1 add_select_fusion.2
  313.4 1.1 add_select_fusion.2
  334.9 1.5 fusion.4
  338.8 81.6 %reduce-scatter.4.cloned.1.call-done = f32[64,512]{1,0:T(8,128)} async-done(((f32[4096,512]{1,0:T(8,128)}), f32[64,512]{1,0:T(8,128)}) %reduce-scatter.4.cloned.1.call-update) | async-done | bytes 131088
  (83 shorter events, 67.2 us)
Async XLA Ops:
  7.2 61.6 %copy-start = (bf16[512,512]{1,0:T(8,128)(2,1)S(1)}, bf16[512,512]{1,0:T(8,128)(2,1)}, u32[]{:S(2)}) copy-start(bf16[512,512]{1,0:T(8,128)(2,1)} %param.7) | copy-start | bytes 1572868
  7.2 55.7 %all-gather.6.cloned.1.call-start = ((), (), s32[]{:S(2)}) async-start(), calls=%async_computation.1 | async-start | bytes 5242880 | tf_op jit(solution)/shard_map/all_gather | solution.py:33
  7.9 158.6 %all-gather.8.cloned.1.call-start = ((), (), s32[]{:S(2)}) async-start(), calls=%async_computation.2 | async-start | bytes 17039360 | tf_op jit(solution)/shard_map/all_gather | solution.py:46
  11.3 58.9 %copy-start.1 = (bf16[512,512]{1,0:T(8,128)(2,1)S(1)}, bf16[512,512]{1,0:T(8,128)(2,1)}, u32[]{:S(2)}) copy-start(bf16[512,512]{1,0:T(8,128)(2,1)} %param.8) | copy-start | bytes 1572868
  11.4 254.8 %all-gather.10.cloned.1.call-start = ((), (), s32[]{:S(2)}) async-start(), calls=%async_computation.3 | async-start | bytes 17039360 | tf_op jit(solution)/shard_map/all_gather | solution.py:12
  69.9 350.4 %reduce-scatter.4.cloned.1.call-start = ((), (), s32[]{:S(2)}) async-start(), calls=%async_computation.4 | async-start | bytes 8519680
  166.5 7.8 %copy-start.2 = (f32[512,4,128]{0,2,1:T(8,128)S(1)}, f32[512,4,128]{0,2,1:T(8,128)}, u32[]{:S(2)}) copy-start(f32[512,4,128]{0,2,1:T(8,128)} %convolution_bitcast_fusion.2) | copy-start | bytes 3145732
Sparse Core Ops, SparseCore 0:
  9.8 53.0 all-gather.5
  66.2 100.2 all-gather.7
  169.9 96.2 all-gather.9
  270.8 149.5 reduce-scatter.3
where the time goes:
time: 429 us; the launch traced here: 427 us
  waiting for transfers between devices  293 us (68%)
  other arithmetic  74.8 us (17%)
  matrix products  27.7 us (6%)
  local copies, waits for them, and re-layouts  15.2 us (4%)
  between operations  13.9 us (3%)
    all_gather x1, waiting for transfers between devices, per_device(): piece = lax.all_gather(kv_term[None], 'seq', axis=0, tiled=True)  89.2 us
    unnamed x5, waiting for transfers between devices  82.3 us
    all_gather x1, waiting for transfers between devices, prefix(): everything = lax.all_gather(shard, axis)  70.1 us
    select_n x64, other arithmetic, turn(): return jnp.where(reached, new, before)  67 us
    all_gather x1, waiting for transfers between devices, per_device(): full_grad = lax.all_gather(out_grad, 'head', axis=1, tiled=True)  51.5 us
    unnamed x10, local copies, waits for them, and re-layouts  13.1 us
  transfers between devices with their start and end apart: 4, of which 4 were waited for; matrix products, arithmetic and copies ran while one was open for 28% of the time, Pallas kernels for 0%

commit v1 on v0

--- a/solution.py
+++ b/solution.py
@@ -3,8 +3,15 @@
 import jax.numpy as jnp
 from jax import lax
 from jax.sharding import PartitionSpec as P
+from jax.lax import all_to_all, axis_size
 
 HD = 128
+
+
+def proceed_terms(a0):
+    frame_out = jnp.stack([a0] * axis_size("head"), axis=0)
+    block_now = all_to_all(frame_out, "head", 0, 0)
+    return jnp.concatenate(block_now, axis=1)
 
 
 def prefix(shard, axis, combine, identity):
@@ -30,7 +37,7 @@
     local_heads = queries.shape[1] // HD
     total = lax.axis_size("seq") * rows
     scale = 1.0 / math.sqrt(HD * total)
-    full_grad = lax.all_gather(out_grad, "head", axis=1, tiled=True)
+    full_grad = proceed_terms(out_grad)
     attn_grad = jnp.dot(full_grad, out_weight, preferred_element_type=jnp.float32).astype(
         jnp.bfloat16
     )

time: 429 us -> 377 us (0.88)
  waiting for transfers between devices: 293 us -> 190 us
  blocking collectives: 0 us -> 52.2 us
    all_to_all x0 -> x1, blocking collectives: none -> 52.2 us  [proceed_terms(): block_now = all_to_all(frame_out, 'head', 0, 0)]
    all_gather x1 -> x0, waiting for transfers between devices: 51.5 us -> none  [per_device(): full_grad = lax.all_gather(out_grad, 'head', axis=1, tiled=True)]
    all_gather x1, waiting for transfers between devices: 89.2 us -> 37.8 us  [per_device(): piece = lax.all_gather(kv_term[None], 'seq', axis=0, tiled=True)]
    unnamed x10 -> x15, local copies, waits for them, and re-layouts: 13.1 us -> 14.6 us
    unnamed x5 -> x4, waiting for transfers between devices: 82.3 us -> 81.7 us
  transfers between devices with their start and end apart: 4 -> 3, of which waited for: 4 -> 3; matrix products, arithmetic and copies ran while one was open for 28% -> 30% of each run, Pallas kernels for 0% -> 0%
where the time goes in v1:
time: 377 us; the launch traced here: 374 us
  waiting for transfers between devices  190 us (50%)
  other arithmetic  74.9 us (20%)
  blocking collectives  52.2 us (14%)
  matrix products  24.3 us (6%)
  local copies, waits for them, and re-layouts  17.1 us (5%)
  between operations  13.9 us (4%)
    unnamed x4, waiting for transfers between devices  81.7 us
    all_gather x1, waiting for transfers between devices, prefix(): everything = lax.all_gather(shard, axis)  70.1 us
    select_n x64, other arithmetic, turn(): return jnp.where(reached, new, before)  67 us
    all_to_all x1, blocking collectives, proceed_terms(): block_now = all_to_all(frame_out, 'head', 0, 0)  52.2 us
    all_gather x1, waiting for transfers between devices, per_device(): piece = lax.all_gather(kv_term[None], 'seq', axis=0, tiled=True)  37.8 us
    unnamed x15, local copies, waits for them, and re-layouts  14.6 us
    dot_general x1, matrix products, per_device(): lax.dot_general(full_grad, flat_out, (((0,), (0,)), ((), ())), preferred_...  8.04 us
    reduce_sum x1, other arithmetic, per_device(): prior_sum = jnp.sum(piece * keep[:, None, None, None], axis=0)  7.74 us
  transfers between devices with their start and end apart: 3, of which 3 were waited for; matrix products, arithmetic and copies ran while one was open for 30% of the time, Pallas kernels for 0%

profile of v1, /device:TPU:2, one launch (start us, length us, event | category | flops | bytes accessed | tf_op | source)
XLA Modules:
  0.0 374.1 jit_solution(15771899275293408792)
XLA Ops:
  7.2 1.3 copy.80
  8.5 2.1 convolution_multiply_fusion.1
  10.7 1.5 copy.52
  12.6 52.2 %all_to_all.5 = bf16[4,512,1024]{1,2,0:T(8,128)(2,1)S(1)} all-to-all(bf16[4,512,1024]{1,2,0:T(8,128)(2,1)S(1)} %stack.2), channel_id=1, replica_groups=mesh['seq'=64,'head'=4] {'head'}, dimensions={0} | all-to-all | bytes 8388608 | tf_op jit(solution)/shard_map/all_to_all | solution.py:13
  64.8 2.4 convolution_convert_fusion
  69.5 1.8 convolution_bitcast_fusion.1
  71.2 1.4 fusion.28
  73.9 1.8 convolution_bitcast_fusion.2
  75.7 37.8 %all-gather.5.cloned.1.call-done = f32[256,128,128]{2,1,0:T(8,128)} async-done(((f32[4,128,128]{2,1,0:T(8,128)}), f32[256,128,128]{2,1,0:T(8,128)}) %all-gather.5.cloned.1.call-update) | async-done | bytes 16777232 | tf_op jit(solution)/shard_map/all_gather | solution.py:53
  113.6 7.7 %multiply_reduce_fusion = bf16[4,128,128]{2,1,0:T(8,128)(2,1)S(1)} fusion(f32[64,4,128,128]{3,2,1,0:T(8,128)} %bitcast.110, f32[64]{0:T(128)S(1)} %compare_convert_fusion), kind=kLoop, calls=%fused_computation.1 | loop fusion | flops 8323072 | bytes 16908544 | tf_op jit(solution)/shard_map/reduce_sum | solution.py:56
  121.3 1.1 fusion.3
  122.4 2.0 copy.70
  124.5 1.6 fusion.6
  126.0 8.0 %multiply_bitcast_fusion = f32[4096,512]{0,1:T(8,128)} fusion(bf16[512,512]{0,1:T(8,128)(2,1)S(1)} %bitcast.119, bf16[512,4096]{0,1:T(8,128)(2,1)} %bitcast.109), kind=kOutput, calls=%fused_computation.2 | convolution fusion | flops 2149580800 | bytes 13107200 | tf_op jit(solution)/shard_map/dot_general | solution.py:85
  134.1 9.0 %copy.78 = f32[4096,512]{1,0:T(8,128)} copy(f32[4096,512]{0,1:T(8,128)} %multiply_bitcast_fusion) | data formatting | bytes 16777216
  143.1 70.1 %all-gather.7.cloned.1.call-done = f32[256,128,128]{2,1,0:T(8,128)} async-done(((f32[4,128,128]{2,1,0:T(8,128)}), f32[256,128,128]{2,1,0:T(8,128)}) %all-gather.7.cloned.1.call-update) | async-done | bytes 16777232 | tf_op jit(solution)/shard_map/all_gather | solution.py:19
  213.2 68.8 %while.16 = (s32[]{:T(128)}, f32[4,128,128]{2,1,0:T(8,128)S(1)}, s32[]{:T(128)}, f32[64,4,128,128]{3,2,1,0:T(8,128)}, s32[]{:T(128)}, /*index=5*/s32[]{:T(128)}, s32[]{:T(128)}, s32[]{:T(128)}) while((s32[]{:T(128)}, f32[4,128,128]{2,1,0:T(8,128)S(1)}, s32[]{:T(128)}, f32[64,4,128,128]{3,2,1,0:T(8,128)}, s32[]{:T(128)}, ...), condition=%wide.region_2.3_spmd.clone, body=%wide.region_1.2_spmd.clone.sunk | while | flops 196616 | bytes 786595 | solution.py:28
  224.9 1.1 add_select_fusion.2
  228.2 1.1 add_select_fusion.2
  248.6 1.1 add_select_fusion.2
  250.8 1.1 add_select_fusion.2
  273.4 1.1 add_select_fusion.2
  282.0 1.6 fusion.5
  285.9 81.7 %reduce-scatter.4.cloned.1.call-done = f32[64,512]{1,0:T(8,128)} async-done(((f32[4096,512]{1,0:T(8,128)}), f32[64,512]{1,0:T(8,128)}) %reduce-scatter.4.cloned.1.call-update) | async-done | bytes 131088
  (87 shorter events, 67.9 us)
Async XLA Ops:
  7.2 60.0 %copy-start = (bf16[512,512]{1,0:T(8,128)(2,1)S(1)}, bf16[512,512]{1,0:T(8,128)(2,1)}, u32[]{:S(2)}) copy-start(bf16[512,512]{1,0:T(8,128)(2,1)} %param.7) | copy-start | bytes 1572868
  7.2 106.4 %all-gather.5.cloned.1.call-start = ((), (), s32[]{:S(2)}) async-start(), calls=%async_computation.2 | async-start | bytes 17039360 | tf_op jit(solution)/shard_map/all_gather | solution.py:53
  10.7 202.5 %all-gather.7.cloned.1.call-start = ((), (), s32[]{:S(2)}) async-start(), calls=%async_computation.3 | async-start | bytes 17039360 | tf_op jit(solution)/shard_map/all_gather | solution.py:19
  12.5 52.2 %copy-start.4 = (bf16[4096,512]{1,0:T(8,128)(2,1)S(1)}, bf16[4096,512]{1,0:T(8,128)(2,1)}, u32[]{:S(2)}) copy-start(bf16[4096,512]{1,0:T(8,128)(2,1)} %param.11) | copy-start | bytes 12582916
  64.8 2.4 copy-start.1
  64.8 3.9 %copy-start.2 = (bf16[512,512]{1,0:T(8,128)(2,1)S(1)}, bf16[512,512]{1,0:T(8,128)(2,1)}, u32[]{:S(2)}) copy-start(bf16[512,512]{1,0:T(8,128)(2,1)} %param.8) | copy-start | bytes 1572868
  68.4 299.2 %reduce-scatter.4.cloned.1.call-start = ((), (), s32[]{:S(2)}) async-start(), calls=%async_computation.4 | async-start | bytes 8519680
  113.6 7.8 %copy-start.3 = (f32[512,4,128]{0,2,1:T(8,128)S(1)}, f32[512,4,128]{0,2,1:T(8,128)}, u32[]{:S(2)}) copy-start(f32[512,4,128]{0,2,1:T(8,128)} %convolution_bitcast_fusion.2) | copy-start | bytes 3145732
Sparse Core Ops, SparseCore 0:
  11.3 102.1 all-gather.4
  116.9 96.2 all-gather.6
  218.0 149.5 reduce-scatter.3
